TPU v7x, 256 devices: a whole 4x4x8 slice. The times are simulated.
256 devices in a mesh: member: 8 (over z_hi, core), lat: 32 (over y, z_lo, x).
Axes of the slice: x: 4, y: 4, z: 8 (z_hi: 4, z_lo: 2; z = z_hi * 2 + z_lo), core: 2. Of those that a mesh axis runs over, the one named last changes fastest.
Arguments:
- ensemble: bfloat16 [16, 64, 128, 256], P('member', None, 'lat'), may hold values from -6 to 6
- cotangent: bfloat16 [16, 64, 128, 256], P('member', None, 'lat'), may hold values from -6 to 6
- conv_in: bfloat16 [3, 3, 64, 128], replicated, may hold values from -0.25 to 0.25
- pool_weight: bfloat16 [256, 128], replicated, may hold values from -1 to 1
- conv_out: bfloat16 [3, 3, 128, 64], replicated, may hold values from -0.1875 to 0.1875
Outputs:
- encoded: bfloat16 [16, 64, 128, 256], P('member', None, 'lat')
- d_input: bfloat16 [16, 64, 128, 256], P('member', None, 'lat')
- grad_conv_in: float32 [3, 3, 64, 128], replicated
- grad_pool: float32 [256, 128], replicated
- grad_conv_out: float32 [3, 3, 128, 64], replicated
All inputs are finite; a program needn't handle non-finite values.
Results may differ from a plain program's by a relative error of at most 0.0085.
Values may be sent and summed in bfloat16 or wider, within the bound.
No kernel may reach another device: no remote copies, remote signals or barrier semaphores. Data moves between devices by JAX's collectives and lax.ppermute only.
A program may use at most 64 MiB of HBM per device.

v0:
```python
import math
import jax
import jax.numpy as jnp
from jax import lax
from jax.sharding import PartitionSpec as P


def padded(cells, sides, width):
    for axis, dim in sides:
        count = lax.axis_size(axis)
        ends = count - 1
        head = lax.slice_in_dim(cells, 0, width, axis=dim)
        tail = lax.slice_in_dim(cells, cells.shape[dim] - width, cells.shape[dim], axis=dim)
        cells = jnp.concatenate(
            [
                lax.ppermute(tail, axis, [(i, (i + 1) % count) for i in range(ends)]),
                cells,
                lax.ppermute(head, axis, [((i + 1) % count, i) for i in range(ends)]),
            ],
            axis=dim,
        )
    return cells


def wrap_longitude(field):
    return jnp.concatenate([field[..., -1:], field, field[..., :1]], axis=3)


def convolve(padded_rows, kernel):
    return lax.conv_general_dilated(
        wrap_longitude(padded_rows),
        kernel,
        (1, 1),
        "VALID",
        dimension_numbers=("NCHW", "HWIO", "NCHW"),
        preferred_element_type=jnp.float32,
    )


def flipped(kernel):
    return jnp.transpose(kernel[::-1, ::-1], (0, 1, 3, 2))


def kernel_grad(padded_rows, output_grad):
    return lax.conv_general_dilated(
        wrap_longitude(padded_rows),
        output_grad,
        (1, 1),
        "VALID",
        dimension_numbers=("CNHW", "IOHW", "HWNC"),
        preferred_element_type=jnp.float32,
    )


def silu_slope(values):
    sigma = jax.nn.sigmoid(values)
    return sigma * (1.0 + values * (1.0 - sigma))


def on_device(ensemble, cotangent, conv_in, pool_weight, conv_out):
    mem_local, var_count, lat_local, lon_count = ensemble.shape
    groups = lax.axis_size("member")
    members = mem_local * groups
    cell_count = lat_local * lon_count
    ens_rows = padded(ensemble, (("lat", 2),), 1)
    pre = convolve(ens_rows, conv_in)
    active = jax.nn.silu(pre).astype(jnp.bfloat16)
    channels = active.shape[1]
    active_cells = active.reshape(mem_local, channels, cell_count)
    active_wide = active_cells.astype(jnp.float32)
    pool_wide = pool_weight.astype(jnp.float32)
    grouped = lax.all_to_all(
        active_cells, "member", split_axis=2, concat_axis=0, tiled=True
    ).astype(jnp.float32)
    local_average = jnp.mean(grouped, axis=0)
    local_spread = jnp.sqrt(jnp.mean((grouped - local_average) ** 2, axis=0) + 0.1)
    local_stats = jnp.concatenate([local_average, local_spread], axis=0)
    local_shared = jnp.dot(pool_wide.T, local_stats, precision=lax.Precision.HIGHEST)
    shared, average, spread = (
        lax.all_gather(local_shared, "member", axis=1, tiled=True),
        lax.all_gather(local_average, "member", axis=1, tiled=True),
        lax.all_gather(local_spread, "member", axis=1, tiled=True),
    )
    zed = active_wide + shared
    hidden = (
        jax.nn.silu(zed).astype(jnp.bfloat16).reshape(mem_local, channels, lat_local, lon_count)
    )
    hid_rows = padded(hidden, (("lat", 2),), 1)
    encoded = (ensemble.astype(jnp.float32) + convolve(hid_rows, conv_out)).astype(jnp.bfloat16)
    cot_rows = padded(cotangent, (("lat", 2),), 1)
    d_hidden = convolve(cot_rows, flipped(conv_out)).reshape(mem_local, channels, cell_count)
    d_zed = (d_hidden * silu_slope(zed)).astype(jnp.bfloat16)
    grad_out = kernel_grad(hid_rows, cotangent)
    zed_grouped = lax.all_to_all(d_zed, "member", split_axis=2, concat_axis=0, tiled=True)
    local_dshared = jnp.sum(zed_grouped.astype(jnp.float32), axis=0)
    local_dstats = jnp.dot(pool_wide, local_dshared, precision=lax.Precision.HIGHEST)
    grad_pool = jnp.dot(local_stats, local_dshared.T, precision=lax.Precision.HIGHEST)
    coef_average = local_dstats[:channels] / members
    coef_spread = local_dstats[channels:] / (members * local_spread)
    coef_average, coef_spread = (
        lax.all_gather(coef_average.astype(jnp.bfloat16), "member", axis=1, tiled=True).astype(
            coef_average.dtype
        ),
        lax.all_gather(coef_spread.astype(jnp.bfloat16), "member", axis=1, tiled=True).astype(
            coef_spread.dtype
        ),
    )
    d_active = d_zed.astype(jnp.float32) + coef_average + coef_spread * (active_wide - average)
    d_pre = (d_active.reshape(mem_local, channels, lat_local, lon_count) * silu_slope(pre)).astype(
        jnp.bfloat16
    )
    dpre_rows = padded(d_pre, (("lat", 2),), 1)
    d_input = (cotangent.astype(jnp.float32) + convolve(dpre_rows, flipped(conv_in))).astype(
        jnp.bfloat16
    )
    grad_in = kernel_grad(ens_rows, d_pre)
    summed = lax.psum((grad_in, grad_pool, grad_out), ("member", "lat"))
    grad_scale = 1.0 / math.sqrt(members * lat_local * lax.axis_size("lat") * lon_count)
    return (
        encoded,
        d_input,
        summed[0] * grad_scale,
        summed[1] * grad_scale,
        summed[2] * grad_scale,
    )


def solution(mesh):
    return jax.shard_map(
        on_device,
        mesh=mesh,
        in_specs=(P("member", None, "lat", None), P("member", None, "lat", None), P(), P(), P()),
        out_specs=(P("member", None, "lat", None), P("member", None, "lat", None), P(), P(), P()),
        check_vma=False,
    )
```

profile of v0, /device:TPU:8, one launch (start us, length us, event | category | flops | bytes accessed | tf_op | source)
XLA Modules:
  0.0 482.6 jit_solution(12388150203696976623)
XLA Ops:
  7.2 1.5 copy.135
  8.9 5.9 %collective-permute-start.1 = (bf16[2,64,1,256]{1,0,3,2:T(2,128)(2,1)S(1)}, bf16[2,64,1,256]{1,0,3,2:T(2,128)(2,1)S(1)}, u32[]{:S(2)}, u32[]{:S(2)}) collective-permute-start(bf16[2,64,1,256]{1,0,3,2:T(2,128)(2,1)S(1)} %get-tuple-element.44), channel_id=1, source_target_pairs={{1,0},{2,1},{3,2},{4,3},{5,4},{6,5},{7,6},{8,7},{9,8},{10,9},{11,1... | collective-permute-start | bytes 196616 | tf_op jit(solution)/shard_map/ppermute | solution.py:18
  14.8 1.9 collective-permute-start
  17.0 6.9 %collective-permute-start.5 = (bf16[2,64,1,256]{3,2,1,0:T(2,128)(2,1)S(1)}, bf16[2,64,1,256]{3,2,1,0:T(2,128)(2,1)S(1)}, u32[]{:S(2)}, u32[]{:S(2)}) collective-permute-start(bf16[2,64,1,256]{3,2,1,0:T(2,128)(2,1)S(1)} %get-tuple-element.46), channel_id=1, source_target_pairs={{1,0},{2,1},{3,2},{4,3},{5,4},{6,5},{7,6},{8,7},{9,8},{10,9},{11,1... | collective-permute-start | bytes 196616 | tf_op jit(solution)/shard_map/ppermute | solution.py:18
  23.9 1.9 collective-permute-start.4
  25.9 8.7 %fusion.81 = bf16[64,6,2,258]{0,2,3,1:T(2,128)(2,1)S(1)} fusion(bf16[2,64,1,256]{1,0,3,2:T(2,128)(2,1)S(1)} %collective-permute-done.1, bf16[2,64,4,256]{1,0,3,2:T(2,128)(2,1)S(1)} %copy.135, bf16[2,64,1,256]{1,0,3,2:T(2,128)(2,1)S(1)} %collective-permute-done), kind=kLoop, calls=%fused_computation.111 | loop fusion | flops 1585152 | bytes 789504 | tf_op jit(solution)/shard_map/concatenate | solution.py:26
  36.2 2.2 add_multiply_fusion
  39.1 1.3 copy.144
  40.5 8.0 %all-to-all-start = ((bf16[2,128,1024]{1,0,2:T(2,128)(2,1)}), bf16[2,128,1024]{1,0,2:T(2,128)(2,1)S(1)}, u32[]{:S(2)}, u32[]{:S(2)}) async-start(bf16[2,128,1024]{1,0,2:T(2,128)(2,1)} %copy.144), calls=%async_computation | async-start | bytes 1048576 | tf_op jit(solution)/shard_map/all_to_all | solution.py:72
  49.1 1.4 maximum_bitcast_fusion
  50.4 1.1 copy.169
  52.4 0.9 fusion.24
  53.3 0.9 convolution_select_fusion.1
  55.6 9.1 %all-to-all-done = bf16[2,128,1024]{1,0,2:T(2,128)(2,1)S(1)} async-done(((bf16[2,128,1024]{1,0,2:T(2,128)(2,1)}), bf16[2,128,1024]{1,0,2:T(2,128)(2,1)S(1)}, u32[]{:S(2)}, u32[]{:S(2)}) %all-to-all-start) | async-done | bytes 524320 | tf_op jit(solution)/shard_map/all_to_all | solution.py:72
  66.9 15.3 %all_gather.12 = f32[128,1024]{0,1:T(8,128)S(1)} all-gather(f32[128,128]{0,1:T(8,128)S(1)} %convolution_bitcast_fusion.1), channel_id=1, replica_groups=mesh['member'=8,'lat'=32] {'member'}, dimensions={1}, use_global_device_ids=true | all-gather | bytes 589824 | tf_op jit(solution)/shard_map/all_gather | solution.py:80
  82.7 1.3 copy.154
  84.1 4.1 all-to-all-start.1
  88.3 1.1 copy.134
  89.3 1.1 copy.148
  90.4 1.2 copy.162
  91.8 1.0 copy-done.11
  93.4 1.0 slice.89
  94.4 27.7 %all_gather.15 = f32[128,1024]{0,1:T(8,128)S(1)} all-gather(f32[128,128]{0,1:T(8,128)S(1)} %copy-done.10), channel_id=1, replica_groups=mesh['member'=8,'lat'=32] {'member'}, dimensions={1}, use_global_device_ids=true | all-gather | bytes 589824 | tf_op jit(solution)/shard_map/all_gather | solution.py:81
  122.1 2.0 copy.155
  124.1 2.0 convert_reduce_fusion
  126.1 2.1 copy.165
  128.2 1.1 reduce_sum.38
  129.6 14.9 %all_gather.14 = bf16[128,1024]{0,1:T(8,128)(2,1)S(1)} all-gather(bf16[128,128]{0,1:T(8,128)(2,1)S(1)} %get-tuple-element.48), channel_id=1, replica_groups=mesh['member'=8,'lat'=32] {'member'}, dimensions={1}, use_global_device_ids=true | all-gather | bytes 294912 | tf_op jit(solution)/shard_map/all_gather | solution.py:104
  144.5 14.6 %all_gather.13 = bf16[128,1024]{0,1:T(8,128)(2,1)S(1)} all-gather(bf16[128,128]{0,1:T(8,128)(2,1)S(1)} %get-tuple-element.47), channel_id=1, replica_groups=mesh['member'=8,'lat'=32] {'member'}, dimensions={1}, use_global_device_ids=true | all-gather | bytes 294912 | tf_op jit(solution)/shard_map/all_gather | solution.py:101
  159.2 3.4 fusion.8
  162.8 7.4 %collective-permute-start.3 = (bf16[2,128,1,256]{1,0,3,2:T(2,128)(2,1)S(1)}, bf16[2,128,1,256]{1,0,3,2:T(2,128)(2,1)S(1)}, u32[]{:S(2)}, u32[]{:S(2)}) collective-permute-start(bf16[2,128,1,256]{1,0,3,2:T(2,128)(2,1)S(1)} %get-tuple-element.42), channel_id=1, source_target_pairs={{1,0},{2,1},{3,2},{4,3},{5,4},{6,5},{7,6},{8,7},{9,8},{10,9},{11,1... | collective-permute-start | bytes 393224 | tf_op jit(solution)/shard_map/ppermute | solution.py:18
  170.3 1.9 collective-permute-start.2
  172.4 6.9 %collective-permute-start.7 = (bf16[2,128,1,256]{1,0,3,2:T(2,128)(2,1)S(1)}, bf16[2,128,1,256]{1,0,3,2:T(2,128)(2,1)S(1)}, u32[]{:S(2)}, u32[]{:S(2)}) collective-permute-start(bf16[2,128,1,256]{1,0,3,2:T(2,128)(2,1)S(1)} %get-tuple-element.38), channel_id=1, source_target_pairs={{1,0},{2,1},{3,2},{4,3},{5,4},{6,5},{7,6},{8,7},{9,8},{10,9},{11,1... | collective-permute-start | bytes 393224 | tf_op jit(solution)/shard_map/ppermute | solution.py:18
  179.3 2.1 collective-permute-start.6
  181.4 4.3 fusion.66
  185.7 1.0 fusion.47
  186.8 7.6 %fusion.80 = bf16[128,6,2,258]{0,2,3,1:T(2,128)(2,1)S(1)} fusion(bf16[2,128,1,256]{1,0,3,2:T(2,128)(2,1)S(1)} %collective-permute-done.3, bf16[2,128,4,256]{1,0,3,2:T(2,128)(2,1)S(1)} %get-tuple-element.34, bf16[2,128,1,256]{1,0,3,2:T(2,128)(2,1)S(1)} %collective-permute-done.2), kind=kLoop, calls=%fused_computation.110 | loop fusion | flops 3170304 | bytes 1579008 | tf_op jit(solution)/shard_map/concatenate | solution.py:26
  195.9 1.4 convolution_select_fusion.2
  197.8 7.8 %fusion.43 = bf16[128,6,2,258]{0,2,3,1:T(2,128)(2,1)S(1)} fusion(bf16[2,128,1,256]{1,0,3,2:T(2,128)(2,1)S(1)} %collective-permute-done.7, bf16[2,128,4,256]{1,0,3,2:T(2,128)(2,1)S(1)} %get-tuple-element.33, bf16[2,128,1,256]{1,0,3,2:T(2,128)(2,1)S(1)} %collective-permute-done.6), kind=kLoop, calls=%fused_computation.74 | loop fusion | flops 3170304 | bytes 1579008 | tf_op jit(solution)/shard_map/concatenate | solution.py:26
  206.5 0.8 copy-done.8
  207.7 4.1 fusion.67
  211.7 1.4 convolution_select_fusion
  213.2 1.0 copy.163
  215.5 1.0 copy.164
  216.5 254.1 %all-reduce.3.cloned.1.call-done = (f32[3,3,64,128]{3,2,1,0:T(8,128)}, f32[256,128]{1,0:T(8,128)}, f32[3,3,128,64]{2,3,1,0:T(8,128)}) async-done(((f32[3,3,64,128]{3,2,1,0:T(8,128)}, f32[256,128]{1,0:T(8,128)}, f32[3,3,128,64]{2,3,1,0:T(8,128)}), (f32[3,3,64,128]{3,2,1,0:T(8,128)}, f32[256,128]{1,0:T(8,128)}, f32[3,3,128,64]{2,3,1,0:T(8,128)})) %all-reduce.3.cloned.1.call-update) | async-done | bytes 720912 | tf_op jit(solution)/shard_map/psum | solution.py:117
  470.6 1.7 broadcast_multiply_fusion.1
  472.3 1.6 broadcast_multiply_fusion.2
  473.9 1.7 broadcast_multiply_fusion
  (105 shorter events, 13.9 us)
Async XLA Ops:
  7.2 28.5 %copy-start = (bf16[3,3,64,128]{3,2,1,0:T(8,128)(2,1)S(1)}, bf16[3,3,64,128]{3,2,1,0:T(8,128)(2,1)}, u32[]{:S(2)}) copy-start(bf16[3,3,64,128]{3,2,1,0:T(8,128)(2,1)} %param.7) | copy-start | bytes 442372
  7.2 9.6 %copy-start.1 = (bf16[2,64,4,256]{3,2,1,0:T(4,128)(2,1)S(1)}, bf16[2,64,4,256]{3,2,1,0:T(4,128)(2,1)}, u32[]{:S(2)}) copy-start(bf16[2,64,4,256]{3,2,1,0:T(4,128)(2,1)} %param.6) | copy-start | bytes 786436
  8.7 25.9 %copy-start.3 = (bf16[2,64,4,256]{1,0,3,2:T(2,128)(2,1)}, bf16[2,64,4,256]{1,0,3,2:T(2,128)(2,1)S(1)}, u32[]{:S(2)}) copy-start(bf16[2,64,4,256]{1,0,3,2:T(2,128)(2,1)S(1)} %copy.135) | copy-start | bytes 786436
  8.9 16.9 %collective-permute-start.1 = (bf16[2,64,1,256]{1,0,3,2:T(2,128)(2,1)S(1)}, bf16[2,64,1,256]{1,0,3,2:T(2,128)(2,1)S(1)}, u32[]{:S(2)}, u32[]{:S(2)}) collective-permute-start(bf16[2,64,1,256]{1,0,3,2:T(2,128)(2,1)S(1)} %get-tuple-element.44), channel_id=1, source_target_pairs={{1,0},{2,1},{3,2},{4,3},{5,4},{6,5},{7,6},{8,7},{9,8},{10,9},{11,1... | collective-permute-start | bytes 196616 | tf_op jit(solution)/shard_map/ppermute | solution.py:18
  14.8 11.0 %collective-permute-start = (bf16[2,64,1,256]{1,0,3,2:T(2,128)(2,1)S(1)}, bf16[2,64,1,256]{1,0,3,2:T(2,128)(2,1)S(1)}, u32[]{:S(2)}, u32[]{:S(2)}) collective-permute-start(bf16[2,64,1,256]{1,0,3,2:T(2,128)(2,1)S(1)} %get-tuple-element.43), channel_id=1, source_target_pairs={{0,1},{1,2},{2,3},{3,4},{4,5},{5,6},{6,7},{7,8},{8,9},{9,10},{10,1... | collective-permute-start | bytes 196616 | tf_op jit(solution)/shard_map/ppermute | solution.py:16
  17.0 31.5 %collective-permute-start.5 = (bf16[2,64,1,256]{3,2,1,0:T(2,128)(2,1)S(1)}, bf16[2,64,1,256]{3,2,1,0:T(2,128)(2,1)S(1)}, u32[]{:S(2)}, u32[]{:S(2)}) collective-permute-start(bf16[2,64,1,256]{3,2,1,0:T(2,128)(2,1)S(1)} %get-tuple-element.46), channel_id=1, source_target_pairs={{1,0},{2,1},{3,2},{4,3},{5,4},{6,5},{7,6},{8,7},{9,8},{10,9},{11,1... | collective-permute-start | bytes 196616 | tf_op jit(solution)/shard_map/ppermute | solution.py:18
  23.9 24.6 %collective-permute-start.4 = (bf16[2,64,1,256]{3,2,1,0:T(2,128)(2,1)S(1)}, bf16[2,64,1,256]{3,2,1,0:T(2,128)(2,1)S(1)}, u32[]{:S(2)}, u32[]{:S(2)}) collective-permute-start(bf16[2,64,1,256]{3,2,1,0:T(2,128)(2,1)S(1)} %get-tuple-element.45), channel_id=1, source_target_pairs={{0,1},{1,2},{2,3},{3,4},{4,5},{5,6},{6,7},{7,8},{8,9},{9,10},{10,1... | collective-permute-start | bytes 196616 | tf_op jit(solution)/shard_map/ppermute | solution.py:16
  25.9 9.6 %copy-start.20 = (bf16[2,64,1,256]{1,0,3,2:T(2,128)(2,1)}, bf16[2,64,1,256]{1,0,3,2:T(2,128)(2,1)S(1)}, u32[]{:S(2)}) copy-start(bf16[2,64,1,256]{1,0,3,2:T(2,128)(2,1)S(1)} %collective-permute-done.1) | copy-start | bytes 196612
  25.9 9.6 %copy-start.22 = (bf16[2,64,1,256]{1,0,3,2:T(2,128)(2,1)}, bf16[2,64,1,256]{1,0,3,2:T(2,128)(2,1)S(1)}, u32[]{:S(2)}) copy-start(bf16[2,64,1,256]{1,0,3,2:T(2,128)(2,1)S(1)} %collective-permute-done) | copy-start | bytes 196612
  35.5 0.7 copy-start.26
  38.3 0.8 copy-start.5
  40.5 24.2 %all-to-all-start = ((bf16[2,128,1024]{1,0,2:T(2,128)(2,1)}), bf16[2,128,1024]{1,0,2:T(2,128)(2,1)S(1)}, u32[]{:S(2)}, u32[]{:S(2)}) async-start(bf16[2,128,1024]{1,0,2:T(2,128)(2,1)} %copy.144), calls=%async_computation | async-start | bytes 1048576 | tf_op jit(solution)/shard_map/all_to_all | solution.py:72
  52.4 1.0 copy-start.24
  64.7 2.0 copy-start.18
  65.2 17.0 %copy-start.9 = (f32[128,128]{0,1:T(8,128)}, f32[128,128]{0,1:T(8,128)S(1)}, u32[]{:S(2)}) copy-start(f32[128,128]{0,1:T(8,128)S(1)} %broadcast_multiply_fusion.3) | copy-start | bytes 196612
  66.0 16.2 %copy-start.15 = (f32[128,128]{0,1:T(8,128)}, f32[128,128]{0,1:T(8,128)S(1)}, u32[]{:S(2)}) copy-start(f32[128,128]{0,1:T(8,128)S(1)} %fusion.13) | copy-start | bytes 196612
  66.1 0.6 copy-start.13
  82.7 5.6 %copy-start.12 = (bf16[2,64,4,256]{3,2,1,0:T(4,128)(2,1)S(1)}, bf16[2,64,4,256]{3,2,1,0:T(4,128)(2,1)}, u32[]{:S(2)}) copy-start(bf16[2,64,4,256]{3,2,1,0:T(4,128)(2,1)} %param.5) | copy-start | bytes 786436
  84.1 38.0 %all-to-all-start.1 = ((bf16[2,128,1024]{1,0,2:T(2,128)(2,1)}), bf16[2,128,1024]{1,0,2:T(2,128)(2,1)}, u32[]{:S(2)}, u32[]{:S(2)}) async-start(bf16[2,128,1024]{1,0,2:T(2,128)(2,1)} %copy.154), calls=%async_computation.1 | async-start | bytes 1048576 | tf_op jit(solution)/shard_map/all_to_all | solution.py:94
  88.2 3.4 copy-start.6
  88.2 382.4 %all-reduce.3.cloned.1.call-start = ((), (), s32[]{:S(2)}) async-start(), calls=%async_computation.2 | async-start | bytes 1441792 | tf_op jit(solution)/shard_map/psum | solution.py:117
  91.6 1.2 copy-start.11
  93.3 1.1 copy-start.10
  126.1 3.2 copy-start.19
  126.1 3.4 copy-start.16
  129.6 29.6 %copy-start.2 = (f32[4,2,256,128]{3,0,2,1:T(4,128)S(1)}, f32[4,2,256,128]{3,0,2,1:T(4,128)}, u32[]{:S(2)}) copy-start(f32[4,2,256,128]{3,0,2,1:T(4,128)} %slice.89) | copy-start | bytes 3145732
  159.2 22.2 %copy-start.4 = (bf16[2,64,4,256]{1,0,3,2:T(2,128)(2,1)S(1)}, bf16[2,64,4,256]{1,0,3,2:T(2,128)(2,1)}, u32[]{:S(2)}) copy-start(bf16[2,64,4,256]{1,0,3,2:T(2,128)(2,1)} %copy-done.3) | copy-start | bytes 786436
  159.2 22.2 %copy-start.21 = (bf16[2,64,1,256]{1,0,3,2:T(2,128)(2,1)S(1)}, bf16[2,64,1,256]{1,0,3,2:T(2,128)(2,1)}, u32[]{:S(2)}) copy-start(bf16[2,64,1,256]{1,0,3,2:T(2,128)(2,1)} %copy-done.20) | copy-start | bytes 196612
  159.2 22.2 %copy-start.23 = (bf16[2,64,1,256]{1,0,3,2:T(2,128)(2,1)S(1)}, bf16[2,64,1,256]{1,0,3,2:T(2,128)(2,1)}, u32[]{:S(2)}) copy-start(bf16[2,64,1,256]{1,0,3,2:T(2,128)(2,1)} %copy-done.22) | copy-start | bytes 196612
  162.8 23.9 %collective-permute-start.3 = (bf16[2,128,1,256]{1,0,3,2:T(2,128)(2,1)S(1)}, bf16[2,128,1,256]{1,0,3,2:T(2,128)(2,1)S(1)}, u32[]{:S(2)}, u32[]{:S(2)}) collective-permute-start(bf16[2,128,1,256]{1,0,3,2:T(2,128)(2,1)S(1)} %get-tuple-element.42), channel_id=1, source_target_pairs={{1,0},{2,1},{3,2},{4,3},{5,4},{6,5},{7,6},{8,7},{9,8},{10,9},{11,1... | collective-permute-start | bytes 393224 | tf_op jit(solution)/shard_map/ppermute | solution.py:18
  170.3 16.5 %collective-permute-start.2 = (bf16[2,128,1,256]{1,0,3,2:T(2,128)(2,1)S(1)}, bf16[2,128,1,256]{1,0,3,2:T(2,128)(2,1)S(1)}, u32[]{:S(2)}, u32[]{:S(2)}) collective-permute-start(bf16[2,128,1,256]{1,0,3,2:T(2,128)(2,1)S(1)} %get-tuple-element.41), channel_id=1, source_target_pairs={{0,1},{1,2},{2,3},{3,4},{4,5},{5,6},{6,7},{7,8},{8,9},{9,10},{10,1... | collective-permute-start | bytes 393224 | tf_op jit(solution)/shard_map/ppermute | solution.py:16
  172.4 25.4 %collective-permute-start.7 = (bf16[2,128,1,256]{1,0,3,2:T(2,128)(2,1)S(1)}, bf16[2,128,1,256]{1,0,3,2:T(2,128)(2,1)S(1)}, u32[]{:S(2)}, u32[]{:S(2)}) collective-permute-start(bf16[2,128,1,256]{1,0,3,2:T(2,128)(2,1)S(1)} %get-tuple-element.38), channel_id=1, source_target_pairs={{1,0},{2,1},{3,2},{4,3},{5,4},{6,5},{7,6},{8,7},{9,8},{10,9},{11,1... | collective-permute-start | bytes 393224 | tf_op jit(solution)/shard_map/ppermute | solution.py:18
  179.3 6.4 %copy-start.14 = (f32[128,128]{0,1:T(8,128)S(1)}, f32[128,128]{0,1:T(8,128)}, u32[]{:S(2)}) copy-start(f32[128,128]{0,1:T(8,128)} %copy-done.13) | copy-start | bytes 196612
  179.3 18.5 %collective-permute-start.6 = (bf16[2,128,1,256]{1,0,3,2:T(2,128)(2,1)S(1)}, bf16[2,128,1,256]{1,0,3,2:T(2,128)(2,1)S(1)}, u32[]{:S(2)}, u32[]{:S(2)}) collective-permute-start(bf16[2,128,1,256]{1,0,3,2:T(2,128)(2,1)S(1)} %get-tuple-element.37), channel_id=1, source_target_pairs={{0,1},{1,2},{2,3},{3,4},{4,5},{5,6},{6,7},{7,8},{8,9},{9,10},{10,1... | collective-permute-start | bytes 393224 | tf_op jit(solution)/shard_map/ppermute | solution.py:16
  195.0 0.9 copy-start.25
  195.0 0.9 copy-start.27
  206.3 1.0 copy-start.8
  206.4 1.2 copy-start.17
  214.2 1.0 copy-start.7
Sparse Core Ops, SparseCore 0:
  211.9 258.6 all-reduce.2
where the time goes:
time: 489 us; the launch traced here: 483 us
  waiting for transfers between devices  263 us (54%)
  blocking collectives  72.5 us (15%)
  starting transfers between devices  47.2 us (10%)
  other arithmetic  40.8 us (8%)
  local copies, waits for them, and re-layouts  28.1 us (6%)
  matrix products  15.8 us (3%)
  between operations  15 us (3%)
    psum x1, waiting for transfers between devices, on_device(): summed = lax.psum((grad_in, grad_pool, grad_out), ('member', 'lat'))  254 us
    all_gather x1, blocking collectives, on_device(): lax.all_gather(local_average, 'member', axis=1, tiled=True)  27.7 us
    ppermute x4, starting transfers between devices, padded(): lax.ppermute(head, axis, [((i + 1) % count, i) for i in range(ends)])  27.2 us
    concatenate x4, other arithmetic, wrap_longitude(): return jnp.concatenate([field[..., -1:], field, field[..., :1]], axis=3)  25.5 us
    unnamed x65, local copies, waits for them, and re-layouts  15.6 us
    all_gather x1, blocking collectives, on_device(): lax.all_gather(local_shared, 'member', axis=1, tiled=True)  15.3 us
    all_gather x1, blocking collectives, on_device(): lax.all_gather(coef_spread.astype(jnp.bfloat16), 'member', axis=1, tiled=...  14.9 us
    all_gather x1, blocking collectives, on_device(): lax.all_gather(coef_average.astype(jnp.bfloat16), 'member', axis=1, tiled...  14.6 us
  transfers between devices with their start and end apart: 11, of which 2 were waited for; matrix products, arithmetic and copies ran while one was open for 9% of the time, Pallas kernels for 0%

commit v1 on v0

--- a/solution.py
+++ b/solution.py
@@ -3,6 +3,13 @@
 import jax.numpy as jnp
 from jax import lax
 from jax.sharding import PartitionSpec as P
+
+
+def exchange_gather(block, axis, dim):
+    count = lax.axis_size(axis)
+    pieces = jnp.stack([block for _ in range(count)])
+    pieces = lax.all_to_all(pieces, axis, split_axis=0, concat_axis=0)
+    return jnp.concatenate(pieces, axis=dim)
 
 
 def padded(cells, sides, width):
@@ -98,9 +105,7 @@
     coef_average = local_dstats[:channels] / members
     coef_spread = local_dstats[channels:] / (members * local_spread)
     coef_average, coef_spread = (
-        lax.all_gather(coef_average.astype(jnp.bfloat16), "member", axis=1, tiled=True).astype(
-            coef_average.dtype
-        ),
+        exchange_gather(coef_average.astype(jnp.bfloat16), "member", 1).astype(coef_average.dtype),
         lax.all_gather(coef_spread.astype(jnp.bfloat16), "member", axis=1, tiled=True).astype(
             coef_spread.dtype
         ),

time: 489 us -> 494 us (1.010)
  blocking collectives: 72.5 us -> 50.2 us
  starting transfers between devices: 47.2 us -> 61.4 us
  waiting for transfers between devices: 263 us -> 275 us
    all_gather x1 -> x0, blocking collectives: 14.6 us -> none  [on_device(): lax.all_gather(coef_average.astype(jnp.bfloat16), 'member', axis=1, tiled...]
    all_to_all x1, waiting for transfers between devices: 0.01 us -> 12.1 us  [on_device(): lax.all_to_all(d_zed, 'member', split_axis=2, concat_axis=0, tiled=True)]
    all_to_all x1, starting transfers between devices: 4.14 us -> 15 us  [on_device(): lax.all_to_all(d_zed, 'member', split_axis=2, concat_axis=0, tiled=True)]
    all_gather x1, blocking collectives: 27.7 us -> 20.2 us  [on_device(): lax.all_gather(local_average, 'member', axis=1, tiled=True)]
  transfers between devices with their start and end apart: 11 -> 12, of which waited for: 2 -> 3; matrix products, arithmetic and copies ran while one was open for 9% -> 10% of each run, Pallas kernels for 0% -> 0%
where the time goes in v1:
time: 494 us; the launch traced here: 487 us
  waiting for transfers between devices  275 us (56%)
  starting transfers between devices  61.4 us (12%)
  blocking collectives  50.2 us (10%)
  other arithmetic  42.7 us (9%)
  local copies, waits for them, and re-layouts  27.2 us (6%)
  matrix products  15.7 us (3%)
  between operations  15 us (3%)
    psum x1, waiting for transfers between devices, on_device(): summed = lax.psum((grad_in, grad_pool, grad_out), ('member', 'lat'))  254 us
    ppermute x4, starting transfers between devices, padded(): lax.ppermute(head, axis, [((i + 1) % count, i) for i in range(ends)])  26.6 us
    concatenate x4, other arithmetic, wrap_longitude(): return jnp.concatenate([field[..., -1:], field, field[..., :1]], axis=3)  25.5 us
    all_gather x1, blocking collectives, on_device(): lax.all_gather(local_average, 'member', axis=1, tiled=True)  20.2 us
    all_gather x1, blocking collectives, on_device(): lax.all_gather(local_shared, 'member', axis=1, tiled=True)  15.3 us
    all_to_all x1, starting transfers between devices, on_device(): lax.all_to_all(d_zed, 'member', split_axis=2, concat_axis=0, tiled=True)  15 us
    unnamed x65, local copies, waits for them, and re-layouts  14.9 us
    all_gather x1, blocking collectives, on_device(): lax.all_gather(coef_spread.astype(jnp.bfloat16), 'member', axis=1, tiled=...  14.6 us
  transfers between devices with their start and end apart: 12, of which 3 were waited for; matrix products, arithmetic and copies ran while one was open for 10% of the time, Pallas kernels for 0%

profile of v1, /device:TPU:8, one launch (start us, length us, event | category | flops | bytes accessed | tf_op | source)
XLA Modules:
  0.0 487.3 jit_solution(13540891283059281398)
XLA Ops:
  7.2 1.5 copy.135
  8.9 5.9 %collective-permute-start.1 = (bf16[2,64,1,256]{1,0,3,2:T(2,128)(2,1)S(1)}, bf16[2,64,1,256]{1,0,3,2:T(2,128)(2,1)S(1)}, u32[]{:S(2)}, u32[]{:S(2)}) collective-permute-start(bf16[2,64,1,256]{1,0,3,2:T(2,128)(2,1)S(1)} %get-tuple-element.44), channel_id=1, source_target_pairs={{1,0},{2,1},{3,2},{4,3},{5,4},{6,5},{7,6},{8,7},{9,8},{10,9},{11,1... | collective-permute-start | bytes 196616 | tf_op jit(solution)/shard_map/ppermute | solution.py:25
  14.8 1.9 collective-permute-start
  17.0 6.9 %collective-permute-start.5 = (bf16[2,64,1,256]{3,2,1,0:T(2,128)(2,1)S(1)}, bf16[2,64,1,256]{3,2,1,0:T(2,128)(2,1)S(1)}, u32[]{:S(2)}, u32[]{:S(2)}) collective-permute-start(bf16[2,64,1,256]{3,2,1,0:T(2,128)(2,1)S(1)} %get-tuple-element.46), channel_id=1, source_target_pairs={{1,0},{2,1},{3,2},{4,3},{5,4},{6,5},{7,6},{8,7},{9,8},{10,9},{11,1... | collective-permute-start | bytes 196616 | tf_op jit(solution)/shard_map/ppermute | solution.py:25
  23.9 1.9 collective-permute-start.4
  25.9 8.7 %fusion.81 = bf16[64,6,2,258]{0,2,3,1:T(2,128)(2,1)S(1)} fusion(bf16[2,64,1,256]{1,0,3,2:T(2,128)(2,1)S(1)} %collective-permute-done.1, bf16[2,64,4,256]{1,0,3,2:T(2,128)(2,1)S(1)} %copy.135, bf16[2,64,1,256]{1,0,3,2:T(2,128)(2,1)S(1)} %collective-permute-done), kind=kLoop, calls=%fused_computation.111 | loop fusion | flops 1585152 | bytes 789504 | tf_op jit(solution)/shard_map/concatenate | solution.py:33
  36.2 2.2 add_multiply_fusion
  39.2 1.3 copy.144
  40.5 8.0 %all-to-all-start = ((bf16[2,128,1024]{1,0,2:T(2,128)(2,1)}), bf16[2,128,1024]{1,0,2:T(2,128)(2,1)S(1)}, u32[]{:S(2)}, u32[]{:S(2)}) async-start(bf16[2,128,1024]{1,0,2:T(2,128)(2,1)} %copy.144), calls=%async_computation | async-start | bytes 1048576 | tf_op jit(solution)/shard_map/all_to_all | solution.py:79
  49.1 1.4 maximum_bitcast_fusion
  50.4 1.1 copy.169
  52.4 0.9 fusion.24
  53.4 0.9 convolution_select_fusion.1
  55.6 9.1 %all-to-all-done = bf16[2,128,1024]{1,0,2:T(2,128)(2,1)S(1)} async-done(((bf16[2,128,1024]{1,0,2:T(2,128)(2,1)}), bf16[2,128,1024]{1,0,2:T(2,128)(2,1)S(1)}, u32[]{:S(2)}, u32[]{:S(2)}) %all-to-all-start) | async-done | bytes 524320 | tf_op jit(solution)/shard_map/all_to_all | solution.py:79
  67.0 15.3 %all_gather.9 = f32[128,1024]{0,1:T(8,128)S(1)} all-gather(f32[128,128]{0,1:T(8,128)S(1)} %convolution_bitcast_fusion.1), channel_id=1, replica_groups=mesh['member'=8,'lat'=32] {'member'}, dimensions={1}, use_global_device_ids=true | all-gather | bytes 589824 | tf_op jit(solution)/shard_map/all_gather | solution.py:87
  82.7 1.3 copy.154
  84.1 15.0 %all-to-all-start.1 = ((bf16[2,128,1024]{1,0,2:T(2,128)(2,1)}), bf16[2,128,1024]{1,0,2:T(2,128)(2,1)S(1)}, u32[]{:S(2)}, u32[]{:S(2)}) async-start(bf16[2,128,1024]{1,0,2:T(2,128)(2,1)} %copy.154), calls=%async_computation.1 | async-start | bytes 1048576 | tf_op jit(solution)/shard_map/all_to_all | solution.py:101
  99.1 1.1 copy.134
  100.2 1.1 copy.148
  101.3 1.2 copy.162
  102.7 1.0 copy-done.11
  104.2 1.0 slice.89
  105.3 12.1 %all-to-all-done.1 = bf16[2,128,1024]{1,0,2:T(2,128)(2,1)S(1)} async-done(((bf16[2,128,1024]{1,0,2:T(2,128)(2,1)}), bf16[2,128,1024]{1,0,2:T(2,128)(2,1)S(1)}, u32[]{:S(2)}, u32[]{:S(2)}) %all-to-all-start.1) | async-done | bytes 524320 | tf_op jit(solution)/shard_map/all_to_all | solution.py:101
  117.4 1.1 copy.155
  118.5 2.0 convert_reduce_fusion
  120.5 1.3 copy.165
  122.9 4.2 all-to-all-start.2
  127.1 20.2 %all_gather.11 = f32[128,1024]{0,1:T(8,128)S(1)} all-gather(f32[128,128]{0,1:T(8,128)S(1)} %copy-done.10), channel_id=1, replica_groups=mesh['member'=8,'lat'=32] {'member'}, dimensions={1}, use_global_device_ids=true | all-gather | bytes 589824 | tf_op jit(solution)/shard_map/all_gather | solution.py:88
  147.3 14.6 %all_gather.10 = bf16[128,1024]{0,1:T(8,128)(2,1)S(1)} all-gather(bf16[128,128]{0,1:T(8,128)(2,1)S(1)} %get-tuple-element.48), channel_id=1, replica_groups=mesh['member'=8,'lat'=32] {'member'}, dimensions={1}, use_global_device_ids=true | all-gather | bytes 294912 | tf_op jit(solution)/shard_map/all_gather | solution.py:109
  162.8 1.0 fusion.47
  163.8 1.0 convert_element_type.101
  165.0 4.6 fusion.8
  169.7 6.8 %collective-permute-start.3 = (bf16[2,128,1,256]{1,0,3,2:T(2,128)(2,1)S(1)}, bf16[2,128,1,256]{1,0,3,2:T(2,128)(2,1)S(1)}, u32[]{:S(2)}, u32[]{:S(2)}) collective-permute-start(bf16[2,128,1,256]{1,0,3,2:T(2,128)(2,1)S(1)} %get-tuple-element.42), channel_id=1, source_target_pairs={{1,0},{2,1},{3,2},{4,3},{5,4},{6,5},{7,6},{8,7},{9,8},{10,9},{11,1... | collective-permute-start | bytes 393224 | tf_op jit(solution)/shard_map/ppermute | solution.py:25
  176.5 1.9 collective-permute-start.2
  178.7 6.9 %collective-permute-start.7 = (bf16[2,128,1,256]{1,0,3,2:T(2,128)(2,1)S(1)}, bf16[2,128,1,256]{1,0,3,2:T(2,128)(2,1)S(1)}, u32[]{:S(2)}, u32[]{:S(2)}) collective-permute-start(bf16[2,128,1,256]{1,0,3,2:T(2,128)(2,1)S(1)} %get-tuple-element.38), channel_id=1, source_target_pairs={{1,0},{2,1},{3,2},{4,3},{5,4},{6,5},{7,6},{8,7},{9,8},{10,9},{11,1... | collective-permute-start | bytes 393224 | tf_op jit(solution)/shard_map/ppermute | solution.py:25
  185.6 1.9 collective-permute-start.6
  187.6 4.3 fusion.66
  191.8 7.6 %fusion.80 = bf16[128,6,2,258]{0,2,3,1:T(2,128)(2,1)S(1)} fusion(bf16[2,128,1,256]{1,0,3,2:T(2,128)(2,1)S(1)} %collective-permute-done.3, bf16[2,128,4,256]{1,0,3,2:T(2,128)(2,1)S(1)} %get-tuple-element.34, bf16[2,128,1,256]{1,0,3,2:T(2,128)(2,1)S(1)} %collective-permute-done.2), kind=kLoop, calls=%fused_computation.110 | loop fusion | flops 3170304 | bytes 1579008 | tf_op jit(solution)/shard_map/concatenate | solution.py:33
  201.0 1.4 convolution_select_fusion.2
  202.9 7.8 %fusion.43 = bf16[128,6,2,258]{0,2,3,1:T(2,128)(2,1)S(1)} fusion(bf16[2,128,1,256]{1,0,3,2:T(2,128)(2,1)S(1)} %collective-permute-done.7, bf16[2,128,4,256]{1,0,3,2:T(2,128)(2,1)S(1)} %get-tuple-element.33, bf16[2,128,1,256]{1,0,3,2:T(2,128)(2,1)S(1)} %collective-permute-done.6), kind=kLoop, calls=%fused_computation.74 | loop fusion | flops 3170304 | bytes 1579008 | tf_op jit(solution)/shard_map/concatenate | solution.py:33
  212.7 4.0 fusion.67
  216.8 1.4 convolution_select_fusion
  218.2 1.0 copy.163
  220.5 1.0 copy.164
  221.5 253.7 %all-reduce.3.cloned.1.call-done = (f32[3,3,64,128]{3,2,1,0:T(8,128)}, f32[256,128]{1,0:T(8,128)}, f32[3,3,128,64]{2,3,1,0:T(8,128)}) async-done(((f32[3,3,64,128]{3,2,1,0:T(8,128)}, f32[256,128]{1,0:T(8,128)}, f32[3,3,128,64]{2,3,1,0:T(8,128)}), (f32[3,3,64,128]{3,2,1,0:T(8,128)}, f32[256,128]{1,0:T(8,128)}, f32[3,3,128,64]{2,3,1,0:T(8,128)})) %all-reduce.3.cloned.1.call-update) | async-done | bytes 720912 | tf_op jit(solution)/shard_map/psum | solution.py:122
  475.3 1.7 broadcast_multiply_fusion.1
  477.0 1.6 broadcast_multiply_fusion.2
  478.5 1.7 broadcast_multiply_fusion
  (107 shorter events, 16.3 us)
Async XLA Ops:
  7.2 28.5 %copy-start = (bf16[3,3,64,128]{3,2,1,0:T(8,128)(2,1)S(1)}, bf16[3,3,64,128]{3,2,1,0:T(8,128)(2,1)}, u32[]{:S(2)}) copy-start(bf16[3,3,64,128]{3,2,1,0:T(8,128)(2,1)} %param.7) | copy-start | bytes 442372
  7.2 9.6 %copy-start.1 = (bf16[2,64,4,256]{3,2,1,0:T(4,128)(2,1)S(1)}, bf16[2,64,4,256]{3,2,1,0:T(4,128)(2,1)}, u32[]{:S(2)}) copy-start(bf16[2,64,4,256]{3,2,1,0:T(4,128)(2,1)} %param.6) | copy-start | bytes 786436
  8.7 25.9 %copy-start.2 = (bf16[2,64,4,256]{1,0,3,2:T(2,128)(2,1)}, bf16[2,64,4,256]{1,0,3,2:T(2,128)(2,1)S(1)}, u32[]{:S(2)}) copy-start(bf16[2,64,4,256]{1,0,3,2:T(2,128)(2,1)S(1)} %copy.135) | copy-start | bytes 786436
  8.9 16.9 %collective-permute-start.1 = (bf16[2,64,1,256]{1,0,3,2:T(2,128)(2,1)S(1)}, bf16[2,64,1,256]{1,0,3,2:T(2,128)(2,1)S(1)}, u32[]{:S(2)}, u32[]{:S(2)}) collective-permute-start(bf16[2,64,1,256]{1,0,3,2:T(2,128)(2,1)S(1)} %get-tuple-element.44), channel_id=1, source_target_pairs={{1,0},{2,1},{3,2},{4,3},{5,4},{6,5},{7,6},{8,7},{9,8},{10,9},{11,1... | collective-permute-start | bytes 196616 | tf_op jit(solution)/shard_map/ppermute | solution.py:25
  14.8 11.0 %collective-permute-start = (bf16[2,64,1,256]{1,0,3,2:T(2,128)(2,1)S(1)}, bf16[2,64,1,256]{1,0,3,2:T(2,128)(2,1)S(1)}, u32[]{:S(2)}, u32[]{:S(2)}) collective-permute-start(bf16[2,64,1,256]{1,0,3,2:T(2,128)(2,1)S(1)} %get-tuple-element.43), channel_id=1, source_target_pairs={{0,1},{1,2},{2,3},{3,4},{4,5},{5,6},{6,7},{7,8},{8,9},{9,10},{10,1... | collective-permute-start | bytes 196616 | tf_op jit(solution)/shard_map/ppermute | solution.py:23
  17.0 31.5 %collective-permute-start.5 = (bf16[2,64,1,256]{3,2,1,0:T(2,128)(2,1)S(1)}, bf16[2,64,1,256]{3,2,1,0:T(2,128)(2,1)S(1)}, u32[]{:S(2)}, u32[]{:S(2)}) collective-permute-start(bf16[2,64,1,256]{3,2,1,0:T(2,128)(2,1)S(1)} %get-tuple-element.46), channel_id=1, source_target_pairs={{1,0},{2,1},{3,2},{4,3},{5,4},{6,5},{7,6},{8,7},{9,8},{10,9},{11,1... | collective-permute-start | bytes 196616 | tf_op jit(solution)/shard_map/ppermute | solution.py:25
  23.9 24.6 %collective-permute-start.4 = (bf16[2,64,1,256]{3,2,1,0:T(2,128)(2,1)S(1)}, bf16[2,64,1,256]{3,2,1,0:T(2,128)(2,1)S(1)}, u32[]{:S(2)}, u32[]{:S(2)}) collective-permute-start(bf16[2,64,1,256]{3,2,1,0:T(2,128)(2,1)S(1)} %get-tuple-element.45), channel_id=1, source_target_pairs={{0,1},{1,2},{2,3},{3,4},{4,5},{5,6},{6,7},{7,8},{8,9},{9,10},{10,1... | collective-permute-start | bytes 196616 | tf_op jit(solution)/shard_map/ppermute | solution.py:23
  25.9 9.6 %copy-start.20 = (bf16[2,64,1,256]{1,0,3,2:T(2,128)(2,1)}, bf16[2,64,1,256]{1,0,3,2:T(2,128)(2,1)S(1)}, u32[]{:S(2)}) copy-start(bf16[2,64,1,256]{1,0,3,2:T(2,128)(2,1)S(1)} %collective-permute-done.1) | copy-start | bytes 196612
  25.9 9.6 %copy-start.22 = (bf16[2,64,1,256]{1,0,3,2:T(2,128)(2,1)}, bf16[2,64,1,256]{1,0,3,2:T(2,128)(2,1)S(1)}, u32[]{:S(2)}) copy-start(bf16[2,64,1,256]{1,0,3,2:T(2,128)(2,1)S(1)} %collective-permute-done) | copy-start | bytes 196612
  35.5 0.7 copy-start.26
  38.4 0.8 copy-start.4
  40.5 24.2 %all-to-all-start = ((bf16[2,128,1024]{1,0,2:T(2,128)(2,1)}), bf16[2,128,1024]{1,0,2:T(2,128)(2,1)S(1)}, u32[]{:S(2)}, u32[]{:S(2)}) async-start(bf16[2,128,1024]{1,0,2:T(2,128)(2,1)} %copy.144), calls=%async_computation | async-start | bytes 1048576 | tf_op jit(solution)/shard_map/all_to_all | solution.py:79
  52.4 1.0 copy-start.24
  64.7 2.0 copy-start.18
  65.3 17.0 %copy-start.9 = (f32[128,128]{0,1:T(8,128)}, f32[128,128]{0,1:T(8,128)S(1)}, u32[]{:S(2)}) copy-start(f32[128,128]{0,1:T(8,128)S(1)} %broadcast_multiply_fusion.3) | copy-start | bytes 196612
  66.1 16.2 %copy-start.15 = (f32[128,128]{0,1:T(8,128)}, f32[128,128]{0,1:T(8,128)S(1)}, u32[]{:S(2)}) copy-start(f32[128,128]{0,1:T(8,128)S(1)} %fusion.13) | copy-start | bytes 196612
  66.1 0.6 copy-start.13
  82.7 16.4 %copy-start.12 = (bf16[2,64,4,256]{3,2,1,0:T(4,128)(2,1)S(1)}, bf16[2,64,4,256]{3,2,1,0:T(4,128)(2,1)}, u32[]{:S(2)}) copy-start(bf16[2,64,4,256]{3,2,1,0:T(4,128)(2,1)} %param.5) | copy-start | bytes 786436
  84.1 33.3 %all-to-all-start.1 = ((bf16[2,128,1024]{1,0,2:T(2,128)(2,1)}), bf16[2,128,1024]{1,0,2:T(2,128)(2,1)S(1)}, u32[]{:S(2)}, u32[]{:S(2)}) async-start(bf16[2,128,1024]{1,0,2:T(2,128)(2,1)} %copy.154), calls=%async_computation.1 | async-start | bytes 1048576 | tf_op jit(solution)/shard_map/all_to_all | solution.py:101
  99.1 3.4 copy-start.5
  102.5 1.2 copy-start.11
  120.5 1.3 copy-start.19
  120.5 1.6 copy-start.16
  121.8 5.3 %copy-start.10 = (f32[128,128]{0,1:T(8,128)S(1)}, f32[128,128]{0,1:T(8,128)}, u32[]{:S(2)}) copy-start(f32[128,128]{0,1:T(8,128)} %copy-done.9) | copy-start | bytes 196612
  122.9 39.9 %copy-start.14 = (f32[128,128]{0,1:T(8,128)S(1)}, f32[128,128]{0,1:T(8,128)}, u32[]{:S(2)}) copy-start(f32[128,128]{0,1:T(8,128)} %copy-done.13) | copy-start | bytes 196612
  122.9 41.0 %all-to-all-start.2 = ((bf16[8,128,128]{1,2,0:T(8,128)(2,1)}), bf16[8,128,128]{1,2,0:T(8,128)(2,1)}, u32[]{:S(2)}, u32[]{:S(2)}) async-start(bf16[8,128,128]{1,2,0:T(8,128)(2,1)} %stack.2), calls=%async_computation.2 | async-start | bytes 524288 | tf_op jit(solution)/shard_map/all_to_all | solution.py:11
  127.0 348.2 %all-reduce.3.cloned.1.call-start = ((), (), s32[]{:S(2)}) async-start(), calls=%async_computation.3 | async-start | bytes 1441792 | tf_op jit(solution)/shard_map/psum | solution.py:122
  163.8 1.1 copy-start.6
  165.0 22.6 %copy-start.3 = (bf16[2,64,4,256]{1,0,3,2:T(2,128)(2,1)S(1)}, bf16[2,64,4,256]{1,0,3,2:T(2,128)(2,1)}, u32[]{:S(2)}) copy-start(bf16[2,64,4,256]{1,0,3,2:T(2,128)(2,1)} %copy-done.2) | copy-start | bytes 786436
  165.0 22.6 %copy-start.21 = (bf16[2,64,1,256]{1,0,3,2:T(2,128)(2,1)S(1)}, bf16[2,64,1,256]{1,0,3,2:T(2,128)(2,1)}, u32[]{:S(2)}) copy-start(bf16[2,64,1,256]{1,0,3,2:T(2,128)(2,1)} %copy-done.20) | copy-start | bytes 196612
  165.0 22.6 %copy-start.23 = (bf16[2,64,1,256]{1,0,3,2:T(2,128)(2,1)S(1)}, bf16[2,64,1,256]{1,0,3,2:T(2,128)(2,1)}, u32[]{:S(2)}) copy-start(bf16[2,64,1,256]{1,0,3,2:T(2,128)(2,1)} %copy-done.22) | copy-start | bytes 196612
  169.7 22.1 %collective-permute-start.3 = (bf16[2,128,1,256]{1,0,3,2:T(2,128)(2,1)S(1)}, bf16[2,128,1,256]{1,0,3,2:T(2,128)(2,1)S(1)}, u32[]{:S(2)}, u32[]{:S(2)}) collective-permute-start(bf16[2,128,1,256]{1,0,3,2:T(2,128)(2,1)S(1)} %get-tuple-element.42), channel_id=1, source_target_pairs={{1,0},{2,1},{3,2},{4,3},{5,4},{6,5},{7,6},{8,7},{9,8},{10,9},{11,1... | collective-permute-start | bytes 393224 | tf_op jit(solution)/shard_map/ppermute | solution.py:25
  176.5 15.3 %collective-permute-start.2 = (bf16[2,128,1,256]{1,0,3,2:T(2,128)(2,1)S(1)}, bf16[2,128,1,256]{1,0,3,2:T(2,128)(2,1)S(1)}, u32[]{:S(2)}, u32[]{:S(2)}) collective-permute-start(bf16[2,128,1,256]{1,0,3,2:T(2,128)(2,1)S(1)} %get-tuple-element.41), channel_id=1, source_target_pairs={{0,1},{1,2},{2,3},{3,4},{4,5},{5,6},{6,7},{7,8},{8,9},{9,10},{10,1... | collective-permute-start | bytes 393224 | tf_op jit(solution)/shard_map/ppermute | solution.py:23
  178.7 24.2 %collective-permute-start.7 = (bf16[2,128,1,256]{1,0,3,2:T(2,128)(2,1)S(1)}, bf16[2,128,1,256]{1,0,3,2:T(2,128)(2,1)S(1)}, u32[]{:S(2)}, u32[]{:S(2)}) collective-permute-start(bf16[2,128,1,256]{1,0,3,2:T(2,128)(2,1)S(1)} %get-tuple-element.38), channel_id=1, source_target_pairs={{1,0},{2,1},{3,2},{4,3},{5,4},{6,5},{7,6},{8,7},{9,8},{10,9},{11,1... | collective-permute-start | bytes 393224 | tf_op jit(solution)/shard_map/ppermute | solution.py:25
  185.6 17.3 %collective-permute-start.6 = (bf16[2,128,1,256]{1,0,3,2:T(2,128)(2,1)S(1)}, bf16[2,128,1,256]{1,0,3,2:T(2,128)(2,1)S(1)}, u32[]{:S(2)}, u32[]{:S(2)}) collective-permute-start(bf16[2,128,1,256]{1,0,3,2:T(2,128)(2,1)S(1)} %get-tuple-element.37), channel_id=1, source_target_pairs={{0,1},{1,2},{2,3},{3,4},{4,5},{5,6},{6,7},{7,8},{8,9},{9,10},{10,1... | collective-permute-start | bytes 393224 | tf_op jit(solution)/shard_map/ppermute | solution.py:23
  200.1 0.9 copy-start.25
  200.1 0.9 copy-start.27
  211.4 1.0 copy-start.8
  211.5 1.2 copy-start.17
  219.2 1.0 copy-start.7
Sparse Core Ops, SparseCore 0:
  216.9 258.2 all-reduce.2
